TPU v7x, 32 devices: a whole 2x2x4 slice. The times are simulated.
32 devices in a mesh: mode: 2 (over x), atom: 16 (over z, y, core).
Axes of the slice: x: 2, y: 2, z: 4, core: 2. Of those that a mesh axis runs over, the one named last changes fastest.
Arguments:
- velocities: bfloat16 [2, 16640, 384], P(None, 'atom'), may hold values from -6 to 6
- flux: bfloat16 [2, 16640, 384], P(None, 'atom'), may hold values from -6 to 6
- atom_ids: int32 [2, 16640], P(None, 'atom'), may hold values from 0 to 16383, as said below
- row_counts: int32 [2, 16], P(None, 'atom'), may hold values from 1008 to 1040, as said below
- vectors: bfloat16 [3, 16384, 1024], P(None, 'atom', 'mode'), may hold values from -0.0390625 to 0.0390625
Outputs:
- correlations: bfloat16 [16, 1024, 1024], P(None, ('mode', 'atom'))
Inputs may be any that keep to these rules, and one draw needn't show every extreme that they name: `atom_ids`: in each frame block the used rows of all domains name every atom 0 to 16383 exactly once; unused rows hold arbitrary atom numbers. One domain holds at most 65 atoms of any one owner block a // 1024, and in every frame block some domain holds exactly 65 atoms of every owner block. `row_counts`: in every frame block the counts sum to 16384 and some domain uses all 1040 rows.
All inputs are finite; a program needn't handle non-finite values.
Results may differ from a plain program's by a relative error of at most 0.0057.
Values may be sent and summed in bfloat16 or wider, within the bound.
No kernel may reach another device: no remote copies, remote signals or barrier semaphores. Data moves between devices by JAX's collectives and lax.ppermute only.
A program may use at most 64 MiB of HBM per device.

v0:
```python
import jax
import jax.numpy as jnp
from jax import lax
from jax.sharding import PartitionSpec as P

LAGS = 16


def body(velocities, flux, atom_ids, row_counts, vectors):
    domains = lax.axis_size("atom")
    blocks = velocities.shape[0]
    dom_rows = velocities.shape[1]
    row_width = 2 * velocities.shape[2]
    frame_len = velocities.shape[2] // 3
    owned_count = vectors.shape[1]
    band_width = vectors.shape[2]
    capacity = dom_rows // domains
    row_index = jnp.arange(dom_rows, dtype=jnp.int32)
    owner_range = jnp.arange(domains, dtype=jnp.int32)

    def project(owned_rows):
        owned_rows = owned_rows.reshape(owned_count, 2, 3, frame_len)
        return jnp.einsum("aqbt,ban->qtn", owned_rows, vectors, preferred_element_type=jnp.float32)

    owned_pieces = []
    for frame_block in range(blocks):
        signals = jnp.concatenate([velocities[frame_block], flux[frame_block]], axis=1)
        live_rows = row_index < row_counts[frame_block, 0]
        owner_ids = atom_ids[frame_block] // owned_count
        local_ids = atom_ids[frame_block] % owned_count
        owner_hits = ((owner_ids[:, None] == owner_range[None, :]) & live_rows[:, None]).astype(
            jnp.int32
        )
        running = jnp.cumsum(owner_hits, axis=0)
        bucket_rank = jnp.sum((running - 1) * owner_hits, axis=1)
        slot_index = jnp.where(live_rows, owner_ids * capacity + bucket_rank, dom_rows)
        outgoing = (
            jnp.zeros((dom_rows, row_width), jnp.bfloat16).at[slot_index].set(signals, mode="drop")
        )
        slot_atoms = jnp.full((dom_rows,), -1, jnp.int32).at[slot_index].set(local_ids, mode="drop")
        outgoing, slot_atoms = (
            outgoing.reshape(domains, capacity, row_width),
            slot_atoms.reshape(domains, capacity),
        )
        arrived, arrived_atoms = (
            lax.all_to_all(outgoing, "atom", split_axis=0, concat_axis=0, tiled=True),
            lax.all_to_all(slot_atoms, "atom", split_axis=0, concat_axis=0, tiled=True),
        )
        target = jnp.where(arrived_atoms >= 0, arrived_atoms, owned_count).reshape(-1)
        owned_pieces.append(
            jnp.zeros((owned_count, row_width), jnp.bfloat16)
            .at[target]
            .set(arrived.reshape(-1, row_width), mode="drop")
        )
    owned_all = jnp.stack(owned_pieces)
    partial_value = jnp.concatenate(
        [project(owned_all[frame_block]) for frame_block in range(blocks)], axis=1
    )
    frames = partial_value.shape[1]
    anchors = frames - LAGS + 1
    own_width = band_width // domains
    own_index = lax.axis_index("atom")
    shares = lax.psum_scatter(partial_value, "atom", scatter_dimension=1, tiled=True)
    heat_share = (shares[0] * shares[1]).astype(jnp.bfloat16)
    heat_series = lax.all_gather(heat_share, "atom", axis=0, tiled=True)
    own_series = lax.dynamic_slice_in_dim(heat_series, own_index * own_width, own_width, 1).T
    lead_series = own_series[:, :anchors]
    lagged = jnp.stack(
        [
            jnp.pad(lead_series, ((0, 0), (lag_index, frames - anchors - lag_index)))
            for lag_index in range(LAGS)
        ]
    )
    lagged = lagged.reshape(LAGS * own_width, frames)
    weighting = 1.0 / anchors
    series_piece = lax.all_gather(heat_series, "mode", axis=1, tiled=True)
    lag_block = jnp.dot(lagged, series_piece, preferred_element_type=jnp.float32) * weighting
    lag_block = lag_block.reshape(LAGS, own_width, series_piece.shape[1])
    return lag_block.astype(jnp.bfloat16)


def solution(mesh):
    in_specs = (
        P(None, "atom", None),
        P(None, "atom", None),
        P(None, "atom"),
        P(None, "atom"),
        P(None, "atom", "mode"),
    )
    out_specs = P(None, ("mode", "atom"), None)
    return jax.shard_map(body, mesh=mesh, in_specs=in_specs, out_specs=out_specs, check_vma=False)
```

profile of v0, /device:TPU:0, one launch (start us, length us, event | category | flops | bytes accessed | tf_op | source)
XLA Modules:
  0.0 277.3 jit_solution(973763235304950492)
XLA Ops:
  6.5 1.4 fusion.46
  9.3 0.8 slice_reduce_fusion.3
  10.3 4.5 %reduce-window.16 = s32[16,9,128]{2,1,0:T(8,128)S(1)} reduce-window(s32[16,9,128]{2,1,0:T(8,128)S(1)} %reshape.339, s32[]{:T(128)} %constant.66.clone.1), window={size=1x1x128 pad=0_0x0_0x127_0}, to_apply=%region_6.7 | reduce-window | flops 2340864 | bytes 147460 | tf_op jit(solution)/shard_map/reduce-window.2
  15.6 4.5 %reduce-window.14 = s32[16,9,128]{2,1,0:T(8,128)S(1)} reduce-window(s32[16,9,128]{2,1,0:T(8,128)S(1)} %reshape.338, s32[]{:T(128)} %constant.66.clone.1), window={size=1x1x128 pad=0_0x0_0x127_0}, to_apply=%region_0.1 | reduce-window | flops 2340864 | bytes 147460 | tf_op jit(solution)/shard_map/reduce-window
  21.0 1.4 fusion.38
  22.4 6.4 %scatter_custom_fusion.3 = s32[1040]{0:T(1024)S(1)} fusion(s32[1040]{0:T(1024)S(1)} %get-tuple-element.6, s32[1040]{0:T(1024)S(1)} %get-tuple-element.15, s32[]{:T(128)} %constant.64.clone.1), kind=kCustom, calls=%fused_computation.113 | custom fusion | bytes 4164 | tf_op jit(solution)/shard_map/scatter | solution.py:40
  29.6 7.4 %all-to-all-start.2 = ((s32[16,1,65]{2,1,0:T(1,128)}), s32[16,1,65]{2,1,0:T(1,128)S(1)}, u32[]{:S(2)}, u32[]{:S(2)}) async-start(s32[16,1,65]{2,1,0:T(1,128)} %all_to_all.26), calls=%async_computation.2 | async-start | bytes 16384 | tf_op jit(solution)/shard_map/all_to_all | solution.py:47
  37.0 6.4 %scatter_custom_fusion = s32[1040]{0:T(1024)S(1)} fusion(s32[1040]{0:T(1024)S(1)} %get-tuple-element.5, s32[1040]{0:T(1024)S(1)} %get-tuple-element.20, s32[]{:T(128)} %constant.64.clone.1), kind=kCustom, calls=%fused_computation.115 | custom fusion | bytes 4164 | tf_op jit(solution)/shard_map/scatter | solution.py:40
  44.1 6.0 %all-to-all-start = ((s32[16,1,65]{2,1,0:T(1,128)}), s32[16,1,65]{2,1,0:T(1,128)S(1)}, u32[]{:S(2)}, u32[]{:S(2)}) async-start(s32[16,1,65]{2,1,0:T(1,128)} %all_to_all.22), calls=%async_computation | async-start | bytes 16384 | tf_op jit(solution)/shard_map/all_to_all | solution.py:47
  50.1 3.6 %slice_bitcast_fusion.2 = (bf16[1040,384]{1,0:T(8,128)(2,1)}, bf16[1040,384]{1,0:T(8,128)(2,1)}, bf16[1040,384]{1,0:T(8,128)(2,1)}, bf16[1040,384]{1,0:T(8,128)(2,1)}) fusion(bf16[2,1040,384]{2,1,0:T(8,128)(2,1)} %param.6, bf16[2,1040,384]{2,1,0:T(8,128)(2,1)} %param.5), kind=kLoop, calls=%fused_computation.24 | loop fusion | bytes 6389760 | tf_op jit(solution)/shard_map/squeeze | solution.py:27
  53.8 10.7 %scatter_custom_fusion.4 = bf16[1040,768]{1,0:T(8,128)(2,1)} fusion(s32[1040]{0:T(1024)S(1)} %get-tuple-element.6, bf16[1040,384]{1,0:T(8,128)(2,1)} %get-tuple-element.12, bf16[]{:T(256)} %constant.142, bf16[1040,384]{1,0:T(8,128)(2,1)} %get-tuple-element.21, bf16[]{:T(256)} %constant.63.clone.1), kind=kCustom, calls=%fused_computation.15 | custom fusion | flops 3194880 | bytes 3194884 | tf_op jit(solution)/shard_map/scatter | solution.py:38
  64.4 2.6 reshape.335
  67.0 6.1 %all-to-all-start.3 = ((bf16[16,65,768]{2,1,0:T(8,128)(2,1)}), bf16[16,65,768]{2,1,0:T(8,128)(2,1)}, u32[]{:S(2)}, u32[]{:S(2)}) async-start(bf16[16,65,768]{2,1,0:T(8,128)(2,1)} %reshape.335), calls=%async_computation.3 | async-start | bytes 3538944 | tf_op jit(solution)/shard_map/all_to_all | solution.py:46
  73.1 10.7 %scatter_custom_fusion.1 = bf16[1040,768]{1,0:T(8,128)(2,1)} fusion(s32[1040]{0:T(1024)S(1)} %get-tuple-element.5, bf16[1040,384]{1,0:T(8,128)(2,1)} %get-tuple-element.11, bf16[]{:T(256)} %constant.142, bf16[1040,384]{1,0:T(8,128)(2,1)} %get-tuple-element.22, bf16[]{:T(256)} %constant.63.clone.1), kind=kCustom, calls=%fused_computation.11 | custom fusion | flops 3194880 | bytes 3194884 | tf_op jit(solution)/shard_map/scatter | solution.py:38
  83.8 2.6 reshape.331
  86.4 22.0 %all-to-all-done.3 = bf16[16,65,768]{2,1,0:T(8,128)(2,1)} async-done(((bf16[16,65,768]{2,1,0:T(8,128)(2,1)}), bf16[16,65,768]{2,1,0:T(8,128)(2,1)}, u32[]{:S(2)}, u32[]{:S(2)}) %all-to-all-start.3) | async-done | bytes 1597472 | tf_op jit(solution)/shard_map/all_to_all | solution.py:46
  108.4 9.9 %all-to-all-start.1 = ((bf16[16,65,768]{2,1,0:T(8,128)(2,1)}), bf16[16,65,768]{2,1,0:T(8,128)(2,1)}, u32[]{:S(2)}, u32[]{:S(2)}) async-start(bf16[16,65,768]{2,1,0:T(8,128)(2,1)} %reshape.331), calls=%async_computation.1 | async-start | bytes 3538944 | tf_op jit(solution)/shard_map/all_to_all | solution.py:46
  120.5 2.6 reshape.384
  123.2 9.9 %scatter_custom_fusion.5 = bf16[1024,768]{1,0:T(8,128)(2,1)} fusion(s32[1040]{0:T(1024)S(1)} %fusion.41, bf16[1040,768]{1,0:T(8,128)(2,1)} %reshape.384, bf16[]{:T(256)} %constant.63.clone.1), kind=kCustom, calls=%fused_computation.28 | custom fusion | bytes 1573376 | tf_op jit(solution)/shard_map/scatter | solution.py:53
  133.1 2.6 copy.12
  135.7 18.0 %all-to-all-done.1 = bf16[16,65,768]{2,1,0:T(8,128)(2,1)} async-done(((bf16[16,65,768]{2,1,0:T(8,128)(2,1)}), bf16[16,65,768]{2,1,0:T(8,128)(2,1)}, u32[]{:S(2)}, u32[]{:S(2)}) %all-to-all-start.1) | async-done | bytes 1597472 | tf_op jit(solution)/shard_map/all_to_all | solution.py:46
  153.7 2.6 reshape.360
  156.3 9.9 %scatter_custom_fusion.2 = bf16[1024,768]{1,0:T(8,128)(2,1)} fusion(s32[1040]{0:T(1024)S(1)} %fusion.39, bf16[1040,768]{1,0:T(8,128)(2,1)} %reshape.360, bf16[]{:T(256)} %constant.63.clone.1), kind=kCustom, calls=%fused_computation.30 | custom fusion | bytes 1573376 | tf_op jit(solution)/shard_map/scatter | solution.py:53
  166.2 2.6 copy.11
  168.8 2.5 fusion.15
  171.3 1.0 fusion.12
  172.3 1.0 pad_maximum_fusion
  173.4 63.1 %reduce-scatter.2.cloned.1.call-done = f32[2,16,512]{2,1,0:T(8,128)} async-done(((f32[2,256,512]{2,1,0:T(8,128)}), f32[2,16,512]{2,1,0:T(8,128)}) %reduce-scatter.2.cloned.1.call-update) | async-done | bytes 65552 | tf_op jit(solution)/shard_map/reduce_scatter | solution.py:63
  236.5 0.8 fusion.33
  237.2 20.1 %all-gather = bf16[1,256,512]{2,1,0:T(8,128)(2,1)S(1)} all-gather(bf16[1,16,512]{2,1,0:T(8,128)(2,1)S(1)} %fusion.33), channel_id=2, replica_groups=mesh['mode'=2,'atom'=16] {'atom'}, dimensions={1}, use_global_device_ids=true | all-gather | bytes 278528 | tf_op jit(solution)/shard_map/all_gather | solution.py:65
  257.3 9.3 %all-gather.1 = bf16[1,256,1024]{2,1,0:T(8,128)(2,1)} all-gather(bf16[1,256,512]{2,1,0:T(8,128)(2,1)S(1)} %all-gather), channel_id=3, replica_groups=mesh['mode'=2,'atom'=16] {'mode'}, dimensions={2}, use_global_device_ids=true | all-gather | bytes 786432 | tf_op jit(solution)/shard_map/all_gather | solution.py:76
  268.0 2.5 multiply_convert_fusion
  (58 shorter events, 7.9 us)
Async XLA Ops:
  6.5 162.3 %copy-start = (bf16[3,1024,512]{2,1,0:T(8,128)(2,1)S(1)}, bf16[3,1024,512]{2,1,0:T(8,128)(2,1)}, u32[]{:S(2)}) copy-start(bf16[3,1024,512]{2,1,0:T(8,128)(2,1)} %param.9) | copy-start | bytes 9437188
  6.5 14.4 %copy-start.2 = (s32[2,1040]{1,0:T(2,128)S(1)}, s32[2,1040]{1,0:T(2,128)}, u32[]{:S(2)}) copy-start(s32[2,1040]{1,0:T(2,128)} %param.7) | copy-start | bytes 24964
  29.6 14.6 %all-to-all-start.2 = ((s32[16,1,65]{2,1,0:T(1,128)}), s32[16,1,65]{2,1,0:T(1,128)S(1)}, u32[]{:S(2)}, u32[]{:S(2)}) async-start(s32[16,1,65]{2,1,0:T(1,128)} %all_to_all.26), calls=%async_computation.2 | async-start | bytes 16384 | tf_op jit(solution)/shard_map/all_to_all | solution.py:47
  44.1 22.9 %all-to-all-start = ((s32[16,1,65]{2,1,0:T(1,128)}), s32[16,1,65]{2,1,0:T(1,128)S(1)}, u32[]{:S(2)}, u32[]{:S(2)}) async-start(s32[16,1,65]{2,1,0:T(1,128)} %all_to_all.22), calls=%async_computation | async-start | bytes 16384 | tf_op jit(solution)/shard_map/all_to_all | solution.py:47
  67.0 41.4 %all-to-all-start.3 = ((bf16[16,65,768]{2,1,0:T(8,128)(2,1)}), bf16[16,65,768]{2,1,0:T(8,128)(2,1)}, u32[]{:S(2)}, u32[]{:S(2)}) async-start(bf16[16,65,768]{2,1,0:T(8,128)(2,1)} %reshape.335), calls=%async_computation.3 | async-start | bytes 3538944 | tf_op jit(solution)/shard_map/all_to_all | solution.py:46
  108.4 45.3 %all-to-all-start.1 = ((bf16[16,65,768]{2,1,0:T(8,128)(2,1)}), bf16[16,65,768]{2,1,0:T(8,128)(2,1)}, u32[]{:S(2)}, u32[]{:S(2)}) async-start(bf16[16,65,768]{2,1,0:T(8,128)(2,1)} %reshape.331), calls=%async_computation.1 | async-start | bytes 3538944 | tf_op jit(solution)/shard_map/all_to_all | solution.py:46
  118.3 118.1 %reduce-scatter.2.cloned.1.call-start = ((), (), s32[]{:S(2)}) async-start(), calls=%async_computation.5 | async-start | bytes 1114112 | tf_op jit(solution)/shard_map/reduce_scatter | solution.py:63
  168.8 2.5 copy-start.1
  173.4 93.4 %copy-start.3 = (pred[256]{0:T(512)(128)(4,1)S(1)}, pred[256]{0:T(512)(128)(4,1)}, u32[]{:S(2)}) copy-start(pred[256]{0:T(512)(128)(4,1)} %constant.62.clone.1) | copy-start | bytes 772
Sparse Core Ops, SparseCore 0:
  173.5 62.9 reduce-scatter.1
where the time goes:
time: 278 us; the launch traced here: 277 us
  waiting for transfers between devices  103 us (37%)
  local copies, waits for them, and re-layouts  58.6 us (21%)
  other arithmetic  37.1 us (13%)
  starting transfers between devices  29.5 us (11%)
  blocking collectives  29.4 us (11%)
  between operations  13.7 us (5%)
  matrix products  5.96 us (2%)
    reduce_scatter x1, waiting for transfers between devices, body(): lax.psum_scatter(partial_value, 'atom', scatter_dimension=1, tiled=True)  63.1 us
    all_to_all x2, waiting for transfers between devices, body(): lax.all_to_all(outgoing, 'atom', split_axis=0, concat_axis=0, tiled=True)  40 us
    scatter x4, local copies, waits for them, and re-layouts, body(): owned_pieces.append(jnp.zeros((owned_count, row_width), jnp.bfloat16).at[...  25 us
    scatter x2, other arithmetic, body(): jnp.zeros((dom_rows, row_width), jnp.bfloat16).at[slot_index]  21.4 us
    all_gather x1, blocking collectives, body(): heat_series = lax.all_gather(heat_share, 'atom', axis=0, tiled=True)  20.1 us
    all_to_all x2, starting transfers between devices, body(): lax.all_to_all(outgoing, 'atom', split_axis=0, concat_axis=0, tiled=True)  16 us
    all_to_all x2, starting transfers between devices, body(): lax.all_to_all(slot_atoms, 'atom', split_axis=0, concat_axis=0, tiled=True)  13.4 us
    scatter x2, local copies, waits for them, and re-layouts, body(): jnp.full((dom_rows,), -1, jnp.int32).at[slot_index]  12.9 us
  transfers between devices with their start and end apart: 5, of which 3 were waited for; matrix products, arithmetic and copies ran while one was open for 19% of the time, Pallas kernels for 0%

commit v1 on v0

--- a/solution.py
+++ b/solution.py
@@ -4,6 +4,28 @@
 from jax.sharding import PartitionSpec as P
 
 LAGS = 16
+
+
+def cut_along(x, dim, size):
+    before, after = (x.shape[:dim], x.shape[dim + 1 :])
+    return jnp.moveaxis(x.reshape(*before, size, -1, *after), dim, 0)
+
+
+def in_order(blocks, dim):
+    lengths = list(blocks.shape[1:])
+    lengths[dim] *= blocks.shape[0]
+    return jnp.moveaxis(blocks, 0, dim).reshape(lengths)
+
+
+def swapped_with_each(x, axis, split_dim, concat_dim):
+    size, index = (lax.axis_size(axis), lax.axis_index(axis))
+    blocks = cut_along(x, split_dim, size)
+    outs = [blocks[index]]
+    for step in range(1, size):
+        sent = blocks[index ^ step]
+        outs.append(lax.ppermute(sent, axis, [(i, i ^ step) for i in range(size)]))
+    blocks = jnp.stack(outs)[index ^ jnp.arange(size)]
+    return in_order(blocks, concat_dim)
 
 
 def body(velocities, flux, atom_ids, row_counts, vectors):
@@ -44,7 +66,7 @@
         )
         arrived, arrived_atoms = (
             lax.all_to_all(outgoing, "atom", split_axis=0, concat_axis=0, tiled=True),
-            lax.all_to_all(slot_atoms, "atom", split_axis=0, concat_axis=0, tiled=True),
+            swapped_with_each(slot_atoms, "atom", 0, 0),
         )
         target = jnp.where(arrived_atoms >= 0, arrived_atoms, owned_count).reshape(-1)
         owned_pieces.append(

time: 278 us -> 302 us (1.086)
  starting transfers between devices: 29.5 us -> 64.3 us
  waiting for transfers between devices: 103 us -> 93.8 us
    ppermute x0 -> x30, starting transfers between devices: none -> 46.9 us  [swapped_with_each(): outs.append(lax.ppermute(sent, axis, [(i, i ^ step) for i in range(size)]))]
    all_to_all x2, waiting for transfers between devices: 40 us -> 22 us  [body(): lax.all_to_all(outgoing, 'atom', split_axis=0, concat_axis=0, tiled=True)]
    ppermute x0 -> x30, waiting for transfers between devices: none -> 14.9 us  [swapped_with_each(): outs.append(lax.ppermute(sent, axis, [(i, i ^ step) for i in range(size)]))]
    all_to_all x2 -> x0, starting transfers between devices: 13.4 us -> none  [body(): lax.all_to_all(slot_atoms, 'atom', split_axis=0, concat_axis=0, tiled=True)]
    reduce_scatter x1, waiting for transfers between devices: 63.1 us -> 56.8 us  [body(): lax.psum_scatter(partial_value, 'atom', scatter_dimension=1, tiled=True)]
  transfers between devices with their start and end apart: 5 -> 33, of which waited for: 3 -> 5; matrix products, arithmetic and copies ran while one was open for 19% -> 14% of each run, Pallas kernels for 0% -> 0%
where the time goes in v1:
time: 302 us
  waiting for transfers between devices  93.8 us (31%)
  starting transfers between devices  64.3 us (21%)
  local copies, waits for them, and re-layouts  58.4 us (19%)
  other arithmetic  35.8 us (12%)
  blocking collectives  29.4 us (10%)
  between operations  13.9 us (5%)
  matrix products  5.96 us (2%)
    reduce_scatter x1, waiting for transfers between devices, body(): lax.psum_scatter(partial_value, 'atom', scatter_dimension=1, tiled=True)  56.8 us
    ppermute x30, starting transfers between devices, swapped_with_each(): outs.append(lax.ppermute(sent, axis, [(i, i ^ step) for i in range(size)]))  46.9 us
    scatter x4, local copies, waits for them, and re-layouts, body(): owned_pieces.append(jnp.zeros((owned_count, row_width), jnp.bfloat16).at[...  25 us
    all_to_all x2, waiting for transfers between devices, body(): lax.all_to_all(outgoing, 'atom', split_axis=0, concat_axis=0, tiled=True)  22 us
    scatter x2, other arithmetic, body(): jnp.zeros((dom_rows, row_width), jnp.bfloat16).at[slot_index]  21.4 us
    all_gather x1, blocking collectives, body(): heat_series = lax.all_gather(heat_share, 'atom', axis=0, tiled=True)  20.1 us
    all_to_all x2, starting transfers between devices, body(): lax.all_to_all(outgoing, 'atom', split_axis=0, concat_axis=0, tiled=True)  17.4 us
    ppermute x30, waiting for transfers between devices, swapped_with_each(): outs.append(lax.ppermute(sent, axis, [(i, i ^ step) for i in range(size)]))  14.9 us
  transfers between devices with their start and end apart: 33, of which 5 were waited for; matrix products, arithmetic and copies ran while one was open for 14% of the time, Pallas kernels for 0%

profile of v1, /device:TPU:0, one launch (start us, length us, event | category | flops | bytes accessed | tf_op | source)
XLA Modules:
  0.0 301.6 jit_solution(14460584885723349137)
XLA Ops:
  10.3 4.5 %reduce-window.16 = s32[16,9,128]{2,1,0:T(8,128)S(1)} reduce-window(s32[16,9,128]{2,1,0:T(8,128)S(1)} %reshape.355, s32[]{:T(128)} %constant.84.clone.1), window={size=1x1x128 pad=0_0x0_0x127_0}, to_apply=%region_6.7 | reduce-window | flops 2340864 | bytes 147460 | tf_op jit(solution)/shard_map/reduce-window.2
  15.6 4.5 %reduce-window.14 = s32[16,9,128]{2,1,0:T(8,128)S(1)} reduce-window(s32[16,9,128]{2,1,0:T(8,128)S(1)} %reshape.354, s32[]{:T(128)} %constant.84.clone.1), window={size=1x1x128 pad=0_0x0_0x127_0}, to_apply=%region_0.1 | reduce-window | flops 2340864 | bytes 147460 | tf_op jit(solution)/shard_map/reduce-window
  22.4 3.6 %slice_bitcast_fusion.2 = (bf16[1040,384]{1,0:T(8,128)(2,1)}, bf16[1040,384]{1,0:T(8,128)(2,1)}, bf16[1040,384]{1,0:T(8,128)(2,1)}, bf16[1040,384]{1,0:T(8,128)(2,1)}) fusion(bf16[2,1040,384]{2,1,0:T(8,128)(2,1)} %param.6, bf16[2,1040,384]{2,1,0:T(8,128)(2,1)} %param.5), kind=kLoop, calls=%fused_computation.26 | loop fusion | bytes 6389760 | tf_op jit(solution)/shard_map/squeeze | solution.py:49
  26.0 10.7 %scatter_custom_fusion.4 = bf16[1040,768]{1,0:T(8,128)(2,1)} fusion(s32[1040]{0:T(1024)S(1)} %get-tuple-element.6, bf16[1040,384]{1,0:T(8,128)(2,1)} %get-tuple-element.12, bf16[]{:T(256)} %constant.170, bf16[1040,384]{1,0:T(8,128)(2,1)} %get-tuple-element.53, bf16[]{:T(256)} %constant.45.clone.1), kind=kCustom, calls=%fused_computation.17 | custom fusion | flops 3194880 | bytes 3194884 | tf_op jit(solution)/shard_map/scatter | solution.py:60
  36.7 2.6 reshape.351
  39.3 7.5 %all-to-all-start.1 = ((bf16[16,65,768]{2,1,0:T(8,128)(2,1)}), bf16[16,65,768]{2,1,0:T(8,128)(2,1)}, u32[]{:S(2)}, u32[]{:S(2)}) async-start(bf16[16,65,768]{2,1,0:T(8,128)(2,1)} %reshape.351), calls=%async_computation.1 | async-start | bytes 3538944 | tf_op jit(solution)/shard_map/all_to_all | solution.py:68
  46.7 10.7 %scatter_custom_fusion.1 = bf16[1040,768]{1,0:T(8,128)(2,1)} fusion(s32[1040]{0:T(1024)S(1)} %get-tuple-element.5, bf16[1040,384]{1,0:T(8,128)(2,1)} %get-tuple-element.11, bf16[]{:T(256)} %constant.170, bf16[1040,384]{1,0:T(8,128)(2,1)} %get-tuple-element.54, bf16[]{:T(256)} %constant.45.clone.1), kind=kCustom, calls=%fused_computation.13 | custom fusion | flops 3194880 | bytes 3194884 | tf_op jit(solution)/shard_map/scatter | solution.py:60
  57.4 2.6 reshape.346
  60.1 22.0 %all-to-all-done.1 = bf16[16,65,768]{2,1,0:T(8,128)(2,1)} async-done(((bf16[16,65,768]{2,1,0:T(8,128)(2,1)}), bf16[16,65,768]{2,1,0:T(8,128)(2,1)}, u32[]{:S(2)}, u32[]{:S(2)}) %all-to-all-start.1) | async-done | bytes 1597472 | tf_op jit(solution)/shard_map/all_to_all | solution.py:68
  82.1 9.9 %all-to-all-start = ((bf16[16,65,768]{2,1,0:T(8,128)(2,1)}), bf16[16,65,768]{2,1,0:T(8,128)(2,1)}, u32[]{:S(2)}, u32[]{:S(2)}) async-start(bf16[16,65,768]{2,1,0:T(8,128)(2,1)} %reshape.346), calls=%async_computation | async-start | bytes 3538944 | tf_op jit(solution)/shard_map/all_to_all | solution.py:68
  92.1 6.6 %scatter_custom_fusion.3 = s32[1040]{0:T(1024)S(1)} fusion(s32[1040]{0:T(1024)S(1)} %get-tuple-element.6, s32[1040]{0:T(1024)S(1)} %get-tuple-element.47, s32[]{:T(128)} %constant.82.clone.1), kind=kCustom, calls=%fused_computation.149 | custom fusion | bytes 4164 | tf_op jit(solution)/shard_map/scatter | solution.py:62
  99.0 4.4 %collective-permute-start.29 = (s32[1,65]{1,0:T(1,128)S(1)}, s32[1,65]{1,0:T(1,128)S(1)}, u32[]{:S(2)}, u32[]{:S(2)}) collective-permute-start(s32[1,65]{1,0:T(1,128)S(1)} %get-tuple-element.31), channel_id=1, source_target_pairs={{0,15},{1,14},{2,13},{3,12},{4,11},{5,10},{6,9},{7,8},{8,7},{9,6},... | collective-permute-start | bytes 788 | tf_op jit(solution)/shard_map/ppermute | solution.py:26
  103.8 3.2 %collective-permute-start.27 = (s32[1,65]{1,0:T(1,128)S(1)}, s32[1,65]{1,0:T(1,128)S(1)}, u32[]{:S(2)}, u32[]{:S(2)}) collective-permute-start(s32[1,65]{1,0:T(1,128)S(1)} %get-tuple-element.33), channel_id=1, source_target_pairs={{0,13},{1,12},{2,15},{3,14},{4,9},{5,8},{6,11},{7,10},{8,5},{9,4},... | collective-permute-start | bytes 788 | tf_op jit(solution)/shard_map/ppermute | solution.py:26
  107.2 6.4 %scatter_custom_fusion = s32[1040]{0:T(1024)S(1)} fusion(s32[1040]{0:T(1024)S(1)} %get-tuple-element.5, s32[1040]{0:T(1024)S(1)} %get-tuple-element.52, s32[]{:T(128)} %constant.82.clone.1), kind=kCustom, calls=%fused_computation.151 | custom fusion | bytes 4164 | tf_op jit(solution)/shard_map/scatter | solution.py:62
  113.9 12.1 %collective-permute-done.29 = s32[1,65]{1,0:T(1,128)S(1)} collective-permute-done((s32[1,65]{1,0:T(1,128)S(1)}, s32[1,65]{1,0:T(1,128)S(1)}, u32[]{:S(2)}, u32[]{:S(2)}) %collective-permute-start.29) | collective-permute-done | bytes 292 | tf_op jit(solution)/shard_map/ppermute | solution.py:26
  126.0 8.9 %collective-permute-start.24 = (s32[1,65]{1,0:T(1,128)S(1)}, s32[1,65]{1,0:T(1,128)S(1)}, u32[]{:S(2)}, u32[]{:S(2)}) collective-permute-start(s32[1,65]{1,0:T(1,128)S(1)} %get-tuple-element.36), channel_id=1, source_target_pairs={{0,10},{1,11},{2,8},{3,9},{4,14},{5,15},{6,12},{7,13},{8,2},{9,3},... | collective-permute-start | bytes 788 | tf_op jit(solution)/shard_map/ppermute | solution.py:26
  135.3 2.3 collective-permute-start.22
  144.0 3.2 %collective-permute-start.14 = (s32[1,65]{1,0:T(1,128)S(1)}, s32[1,65]{1,0:T(1,128)S(1)}, u32[]{:S(2)}, u32[]{:S(2)}) collective-permute-start(s32[1,65]{1,0:T(1,128)S(1)} %get-tuple-element.13), channel_id=1, source_target_pairs={{0,15},{1,14},{2,13},{3,12},{4,11},{5,10},{6,9},{7,8},{8,7},{9,6},... | collective-permute-start | bytes 788 | tf_op jit(solution)/shard_map/ppermute | solution.py:26
  152.7 3.9 %collective-permute-start.9 = (s32[1,65]{1,0:T(1,128)S(1)}, s32[1,65]{1,0:T(1,128)S(1)}, u32[]{:S(2)}, u32[]{:S(2)}) collective-permute-start(s32[1,65]{1,0:T(1,128)S(1)} %get-tuple-element.18), channel_id=1, source_target_pairs={{0,10},{1,11},{2,8},{3,9},{4,14},{5,15},{6,12},{7,13},{8,2},{9,3},... | collective-permute-start | bytes 788 | tf_op jit(solution)/shard_map/ppermute | solution.py:26
  156.6 2.3 collective-permute-start.7
  166.3 1.9 collective-permute-done.1
  169.0 2.6 reshape.420
  171.7 9.9 %scatter_custom_fusion.5 = bf16[1024,768]{1,0:T(8,128)(2,1)} fusion(s32[1040]{0:T(1024)S(1)} %fusion.41, bf16[1040,768]{1,0:T(8,128)(2,1)} %reshape.420, bf16[]{:T(256)} %constant.45.clone.1), kind=kCustom, calls=%fused_computation.30 | custom fusion | bytes 1573376 | tf_op jit(solution)/shard_map/scatter | solution.py:75
  181.6 2.6 copy.99
  184.2 2.6 reshape.396
  186.8 9.9 %scatter_custom_fusion.2 = bf16[1024,768]{1,0:T(8,128)(2,1)} fusion(s32[1040]{0:T(1024)S(1)} %fusion.39, bf16[1040,768]{1,0:T(8,128)(2,1)} %reshape.396, bf16[]{:T(256)} %constant.45.clone.1), kind=kCustom, calls=%fused_computation.32 | custom fusion | bytes 1573376 | tf_op jit(solution)/shard_map/scatter | solution.py:75
  196.7 2.6 copy.83
  199.3 2.5 fusion.15
  203.9 56.8 %reduce-scatter.2.cloned.1.call-done = f32[2,16,512]{2,1,0:T(8,128)} async-done(((f32[2,256,512]{2,1,0:T(8,128)}), f32[2,16,512]{2,1,0:T(8,128)}) %reduce-scatter.2.cloned.1.call-update) | async-done | bytes 65552 | tf_op jit(solution)/shard_map/reduce_scatter | solution.py:85
  261.5 20.1 %all-gather = bf16[1,256,512]{2,1,0:T(8,128)(2,1)S(1)} all-gather(bf16[1,16,512]{2,1,0:T(8,128)(2,1)S(1)} %fusion.33), channel_id=2, replica_groups=mesh['mode'=2,'atom'=16] {'atom'}, dimensions={1}, use_global_device_ids=true | all-gather | bytes 278528 | tf_op jit(solution)/shard_map/all_gather | solution.py:87
  281.6 9.3 %all-gather.1 = bf16[1,256,1024]{2,1,0:T(8,128)(2,1)} all-gather(bf16[1,256,512]{2,1,0:T(8,128)(2,1)S(1)} %all-gather), channel_id=3, replica_groups=mesh['mode'=2,'atom'=16] {'mode'}, dimensions={2}, use_global_device_ids=true | all-gather | bytes 786432 | tf_op jit(solution)/shard_map/all_gather | solution.py:98
  292.3 2.5 multiply_convert_fusion
  (119 shorter events, 32.3 us)
Async XLA Ops:
  39.3 42.8 %all-to-all-start.1 = ((bf16[16,65,768]{2,1,0:T(8,128)(2,1)}), bf16[16,65,768]{2,1,0:T(8,128)(2,1)}, u32[]{:S(2)}, u32[]{:S(2)}) async-start(bf16[16,65,768]{2,1,0:T(8,128)(2,1)} %reshape.351), calls=%async_computation.1 | async-start | bytes 3538944 | tf_op jit(solution)/shard_map/all_to_all | solution.py:68
  82.1 102.1 %all-to-all-start = ((bf16[16,65,768]{2,1,0:T(8,128)(2,1)}), bf16[16,65,768]{2,1,0:T(8,128)(2,1)}, u32[]{:S(2)}, u32[]{:S(2)}) async-start(bf16[16,65,768]{2,1,0:T(8,128)(2,1)} %reshape.346), calls=%async_computation | async-start | bytes 3538944 | tf_op jit(solution)/shard_map/all_to_all | solution.py:68
  92.0 168.7 %reduce-scatter.2.cloned.1.call-start = ((), (), s32[]{:S(2)}) async-start(), calls=%async_computation.3 | async-start | bytes 1114112 | tf_op jit(solution)/shard_map/reduce_scatter | solution.py:85
  99.0 26.9 %collective-permute-start.29 = (s32[1,65]{1,0:T(1,128)S(1)}, s32[1,65]{1,0:T(1,128)S(1)}, u32[]{:S(2)}, u32[]{:S(2)}) collective-permute-start(s32[1,65]{1,0:T(1,128)S(1)} %get-tuple-element.31), channel_id=1, source_target_pairs={{0,15},{1,14},{2,13},{3,12},{4,11},{5,10},{6,9},{7,8},{8,7},{9,6},... | collective-permute-start | bytes 788 | tf_op jit(solution)/shard_map/ppermute | solution.py:26
  103.4 31.5 %collective-permute-start.28 = (s32[1,65]{1,0:T(1,128)S(1)}, s32[1,65]{1,0:T(1,128)S(1)}, u32[]{:S(2)}, u32[]{:S(2)}) collective-permute-start(s32[1,65]{1,0:T(1,128)S(1)} %get-tuple-element.32), channel_id=1, source_target_pairs={{0,14},{1,15},{2,12},{3,13},{4,10},{5,11},{6,8},{7,9},{8,6},{9,7},... | collective-permute-start | bytes 788 | tf_op jit(solution)/shard_map/ppermute | solution.py:26
  103.8 31.5 %collective-permute-start.27 = (s32[1,65]{1,0:T(1,128)S(1)}, s32[1,65]{1,0:T(1,128)S(1)}, u32[]{:S(2)}, u32[]{:S(2)}) collective-permute-start(s32[1,65]{1,0:T(1,128)S(1)} %get-tuple-element.33), channel_id=1, source_target_pairs={{0,13},{1,12},{2,15},{3,14},{4,9},{5,8},{6,11},{7,10},{8,5},{9,4},... | collective-permute-start | bytes 788 | tf_op jit(solution)/shard_map/ppermute | solution.py:26
  106.9 30.7 %collective-permute-start.26 = (s32[1,65]{1,0:T(1,128)S(1)}, s32[1,65]{1,0:T(1,128)S(1)}, u32[]{:S(2)}, u32[]{:S(2)}) collective-permute-start(s32[1,65]{1,0:T(1,128)S(1)} %get-tuple-element.34), channel_id=1, source_target_pairs={{0,12},{1,13},{2,14},{3,15},{4,8},{5,9},{6,10},{7,11},{8,4},{9,5},... | collective-permute-start | bytes 788 | tf_op jit(solution)/shard_map/ppermute | solution.py:26
  107.2 31.4 %collective-permute-start.25 = (s32[1,65]{1,0:T(1,128)S(1)}, s32[1,65]{1,0:T(1,128)S(1)}, u32[]{:S(2)}, u32[]{:S(2)}) collective-permute-start(s32[1,65]{1,0:T(1,128)S(1)} %get-tuple-element.35), channel_id=1, source_target_pairs={{0,11},{1,10},{2,9},{3,8},{4,15},{5,14},{6,13},{7,12},{8,3},{9,2},... | collective-permute-start | bytes 788 | tf_op jit(solution)/shard_map/ppermute | solution.py:26
  126.0 14.3 %collective-permute-start.24 = (s32[1,65]{1,0:T(1,128)S(1)}, s32[1,65]{1,0:T(1,128)S(1)}, u32[]{:S(2)}, u32[]{:S(2)}) collective-permute-start(s32[1,65]{1,0:T(1,128)S(1)} %get-tuple-element.36), channel_id=1, source_target_pairs={{0,10},{1,11},{2,8},{3,9},{4,14},{5,15},{6,12},{7,13},{8,2},{9,3},... | collective-permute-start | bytes 788 | tf_op jit(solution)/shard_map/ppermute | solution.py:26
  134.9 5.8 %collective-permute-start.23 = (s32[1,65]{1,0:T(1,128)S(1)}, s32[1,65]{1,0:T(1,128)S(1)}, u32[]{:S(2)}, u32[]{:S(2)}) collective-permute-start(s32[1,65]{1,0:T(1,128)S(1)} %get-tuple-element.37), channel_id=1, source_target_pairs={{0,9},{1,8},{2,11},{3,10},{4,13},{5,12},{6,15},{7,14},{8,1},{9,0},... | collective-permute-start | bytes 788 | tf_op jit(solution)/shard_map/ppermute | solution.py:26
  135.3 6.7 %collective-permute-start.22 = (s32[1,65]{1,0:T(1,128)S(1)}, s32[1,65]{1,0:T(1,128)S(1)}, u32[]{:S(2)}, u32[]{:S(2)}) collective-permute-start(s32[1,65]{1,0:T(1,128)S(1)} %get-tuple-element.38), channel_id=1, source_target_pairs={{0,8},{1,9},{2,10},{3,11},{4,12},{5,13},{6,14},{7,15},{8,0},{9,1},... | collective-permute-start | bytes 788 | tf_op jit(solution)/shard_map/ppermute | solution.py:26
  137.6 5.5 %collective-permute-start.21 = (s32[1,65]{1,0:T(1,128)S(1)}, s32[1,65]{1,0:T(1,128)S(1)}, u32[]{:S(2)}, u32[]{:S(2)}) collective-permute-start(s32[1,65]{1,0:T(1,128)S(1)} %get-tuple-element.39), channel_id=1, source_target_pairs={{0,7},{1,6},{2,5},{3,4},{4,3},{5,2},{6,1},{7,0},{8,15},{9,14},{10,... | collective-permute-start | bytes 788 | tf_op jit(solution)/shard_map/ppermute | solution.py:26
  138.6 5.3 %collective-permute-start.20 = (s32[1,65]{1,0:T(1,128)S(1)}, s32[1,65]{1,0:T(1,128)S(1)}, u32[]{:S(2)}, u32[]{:S(2)}) collective-permute-start(s32[1,65]{1,0:T(1,128)S(1)} %get-tuple-element.40), channel_id=1, source_target_pairs={{0,6},{1,7},{2,4},{3,5},{4,2},{5,3},{6,0},{7,1},{8,14},{9,15},{10,... | collective-permute-start | bytes 788 | tf_op jit(solution)/shard_map/ppermute | solution.py:26
  140.2 3.8 %collective-permute-start.19 = (s32[1,65]{1,0:T(1,128)S(1)}, s32[1,65]{1,0:T(1,128)S(1)}, u32[]{:S(2)}, u32[]{:S(2)}) collective-permute-start(s32[1,65]{1,0:T(1,128)S(1)} %get-tuple-element.41), channel_id=1, source_target_pairs={{0,5},{1,4},{2,7},{3,6},{4,1},{5,0},{6,3},{7,2},{8,13},{9,12},{10,... | collective-permute-start | bytes 788 | tf_op jit(solution)/shard_map/ppermute | solution.py:26
  140.7 6.5 %collective-permute-start.18 = (s32[1,65]{1,0:T(1,128)S(1)}, s32[1,65]{1,0:T(1,128)S(1)}, u32[]{:S(2)}, u32[]{:S(2)}) collective-permute-start(s32[1,65]{1,0:T(1,128)S(1)} %get-tuple-element.42), channel_id=1, source_target_pairs={{0,4},{1,5},{2,6},{3,7},{4,0},{5,1},{6,2},{7,3},{8,12},{9,13},{10,... | collective-permute-start | bytes 788 | tf_op jit(solution)/shard_map/ppermute | solution.py:26
  142.0 6.7 %collective-permute-start.17 = (s32[1,65]{1,0:T(1,128)S(1)}, s32[1,65]{1,0:T(1,128)S(1)}, u32[]{:S(2)}, u32[]{:S(2)}) collective-permute-start(s32[1,65]{1,0:T(1,128)S(1)} %get-tuple-element.43), channel_id=1, source_target_pairs={{0,3},{1,2},{2,1},{3,0},{4,7},{5,6},{6,5},{7,4},{8,11},{9,10},{10,... | collective-permute-start | bytes 788 | tf_op jit(solution)/shard_map/ppermute | solution.py:26
  143.1 7.4 %collective-permute-start.16 = (s32[1,65]{1,0:T(1,128)S(1)}, s32[1,65]{1,0:T(1,128)S(1)}, u32[]{:S(2)}, u32[]{:S(2)}) collective-permute-start(s32[1,65]{1,0:T(1,128)S(1)} %get-tuple-element.44), channel_id=1, source_target_pairs={{0,2},{1,3},{2,0},{3,1},{4,6},{5,7},{6,4},{7,5},{8,10},{9,11},{10,... | collective-permute-start | bytes 788 | tf_op jit(solution)/shard_map/ppermute | solution.py:26
  143.9 8.1 %collective-permute-start.15 = (s32[1,65]{1,0:T(1,128)S(1)}, s32[1,65]{1,0:T(1,128)S(1)}, u32[]{:S(2)}, u32[]{:S(2)}) collective-permute-start(s32[1,65]{1,0:T(1,128)S(1)} %get-tuple-element.45), channel_id=1, source_target_pairs={{0,1},{1,0},{2,3},{3,2},{4,5},{5,4},{6,7},{7,6},{8,9},{9,8},{10,11... | collective-permute-start | bytes 788 | tf_op jit(solution)/shard_map/ppermute | solution.py:26
  144.0 8.6 %collective-permute-start.14 = (s32[1,65]{1,0:T(1,128)S(1)}, s32[1,65]{1,0:T(1,128)S(1)}, u32[]{:S(2)}, u32[]{:S(2)}) collective-permute-start(s32[1,65]{1,0:T(1,128)S(1)} %get-tuple-element.13), channel_id=1, source_target_pairs={{0,15},{1,14},{2,13},{3,12},{4,11},{5,10},{6,9},{7,8},{8,7},{9,6},... | collective-permute-start | bytes 788 | tf_op jit(solution)/shard_map/ppermute | solution.py:26
  147.2 9.4 %collective-permute-start.13 = (s32[1,65]{1,0:T(1,128)S(1)}, s32[1,65]{1,0:T(1,128)S(1)}, u32[]{:S(2)}, u32[]{:S(2)}) collective-permute-start(s32[1,65]{1,0:T(1,128)S(1)} %get-tuple-element.14), channel_id=1, source_target_pairs={{0,14},{1,15},{2,12},{3,13},{4,10},{5,11},{6,8},{7,9},{8,6},{9,7},... | collective-permute-start | bytes 788 | tf_op jit(solution)/shard_map/ppermute | solution.py:26
  148.8 7.8 %collective-permute-start.12 = (s32[1,65]{1,0:T(1,128)S(1)}, s32[1,65]{1,0:T(1,128)S(1)}, u32[]{:S(2)}, u32[]{:S(2)}) collective-permute-start(s32[1,65]{1,0:T(1,128)S(1)} %get-tuple-element.15), channel_id=1, source_target_pairs={{0,13},{1,12},{2,15},{3,14},{4,9},{5,8},{6,11},{7,10},{8,5},{9,4},... | collective-permute-start | bytes 788 | tf_op jit(solution)/shard_map/ppermute | solution.py:26
  150.5 8.4 %collective-permute-start.11 = (s32[1,65]{1,0:T(1,128)S(1)}, s32[1,65]{1,0:T(1,128)S(1)}, u32[]{:S(2)}, u32[]{:S(2)}) collective-permute-start(s32[1,65]{1,0:T(1,128)S(1)} %get-tuple-element.16), channel_id=1, source_target_pairs={{0,12},{1,13},{2,14},{3,15},{4,8},{5,9},{6,10},{7,11},{8,4},{9,5},... | collective-permute-start | bytes 788 | tf_op jit(solution)/shard_map/ppermute | solution.py:26
  152.0 8.0 %collective-permute-start.10 = (s32[1,65]{1,0:T(1,128)S(1)}, s32[1,65]{1,0:T(1,128)S(1)}, u32[]{:S(2)}, u32[]{:S(2)}) collective-permute-start(s32[1,65]{1,0:T(1,128)S(1)} %get-tuple-element.17), channel_id=1, source_target_pairs={{0,11},{1,10},{2,9},{3,8},{4,15},{5,14},{6,13},{7,12},{8,3},{9,2},... | collective-permute-start | bytes 788 | tf_op jit(solution)/shard_map/ppermute | solution.py:26
  152.7 9.2 %collective-permute-start.9 = (s32[1,65]{1,0:T(1,128)S(1)}, s32[1,65]{1,0:T(1,128)S(1)}, u32[]{:S(2)}, u32[]{:S(2)}) collective-permute-start(s32[1,65]{1,0:T(1,128)S(1)} %get-tuple-element.18), channel_id=1, source_target_pairs={{0,10},{1,11},{2,8},{3,9},{4,14},{5,15},{6,12},{7,13},{8,2},{9,3},... | collective-permute-start | bytes 788 | tf_op jit(solution)/shard_map/ppermute | solution.py:26
  156.5 5.3 %collective-permute-start.8 = (s32[1,65]{1,0:T(1,128)S(1)}, s32[1,65]{1,0:T(1,128)S(1)}, u32[]{:S(2)}, u32[]{:S(2)}) collective-permute-start(s32[1,65]{1,0:T(1,128)S(1)} %get-tuple-element.19), channel_id=1, source_target_pairs={{0,9},{1,8},{2,11},{3,10},{4,13},{5,12},{6,15},{7,14},{8,1},{9,0},... | collective-permute-start | bytes 788 | tf_op jit(solution)/shard_map/ppermute | solution.py:26
  156.6 6.8 %collective-permute-start.7 = (s32[1,65]{1,0:T(1,128)S(1)}, s32[1,65]{1,0:T(1,128)S(1)}, u32[]{:S(2)}, u32[]{:S(2)}) collective-permute-start(s32[1,65]{1,0:T(1,128)S(1)} %get-tuple-element.20), channel_id=1, source_target_pairs={{0,8},{1,9},{2,10},{3,11},{4,12},{5,13},{6,14},{7,15},{8,0},{9,1},... | collective-permute-start | bytes 788 | tf_op jit(solution)/shard_map/ppermute | solution.py:26
  158.9 5.8 %collective-permute-start.6 = (s32[1,65]{1,0:T(1,128)S(1)}, s32[1,65]{1,0:T(1,128)S(1)}, u32[]{:S(2)}, u32[]{:S(2)}) collective-permute-start(s32[1,65]{1,0:T(1,128)S(1)} %get-tuple-element.21), channel_id=1, source_target_pairs={{0,7},{1,6},{2,5},{3,4},{4,3},{5,2},{6,1},{7,0},{8,15},{9,14},{10,... | collective-permute-start | bytes 788 | tf_op jit(solution)/shard_map/ppermute | solution.py:26
  160.1 5.3 %collective-permute-start.5 = (s32[1,65]{1,0:T(1,128)S(1)}, s32[1,65]{1,0:T(1,128)S(1)}, u32[]{:S(2)}, u32[]{:S(2)}) collective-permute-start(s32[1,65]{1,0:T(1,128)S(1)} %get-tuple-element.22), channel_id=1, source_target_pairs={{0,6},{1,7},{2,4},{3,5},{4,2},{5,3},{6,0},{7,1},{8,14},{9,15},{10,... | collective-permute-start | bytes 788 | tf_op jit(solution)/shard_map/ppermute | solution.py:26
  161.8 3.6 %collective-permute-start.4 = (s32[1,65]{1,0:T(1,128)S(1)}, s32[1,65]{1,0:T(1,128)S(1)}, u32[]{:S(2)}, u32[]{:S(2)}) collective-permute-start(s32[1,65]{1,0:T(1,128)S(1)} %get-tuple-element.23), channel_id=1, source_target_pairs={{0,5},{1,4},{2,7},{3,6},{4,1},{5,0},{6,3},{7,2},{8,13},{9,12},{10,... | collective-permute-start | bytes 788 | tf_op jit(solution)/shard_map/ppermute | solution.py:26
  161.9 3.6 %collective-permute-start.3 = (s32[1,65]{1,0:T(1,128)S(1)}, s32[1,65]{1,0:T(1,128)S(1)}, u32[]{:S(2)}, u32[]{:S(2)}) collective-permute-start(s32[1,65]{1,0:T(1,128)S(1)} %get-tuple-element.24), channel_id=1, source_target_pairs={{0,4},{1,5},{2,6},{3,7},{4,0},{5,1},{6,2},{7,3},{8,12},{9,13},{10,... | collective-permute-start | bytes 788 | tf_op jit(solution)/shard_map/ppermute | solution.py:26
  163.3 3.0 collective-permute-start.2
  164.7 3.6 %collective-permute-start.1 = (s32[1,65]{1,0:T(1,128)S(1)}, s32[1,65]{1,0:T(1,128)S(1)}, u32[]{:S(2)}, u32[]{:S(2)}) collective-permute-start(s32[1,65]{1,0:T(1,128)S(1)} %get-tuple-element.26), channel_id=1, source_target_pairs={{0,2},{1,3},{2,0},{3,1},{4,6},{5,7},{6,4},{7,5},{8,10},{9,11},{10,... | collective-permute-start | bytes 788 | tf_op jit(solution)/shard_map/ppermute | solution.py:26
  (5 other events, 299.8 us)
Sparse Core Ops, SparseCore 0:
  204.0 56.6 reduce-scatter.1
